TPU v7x, 32 devices: a whole 2x2x4 slice. The times are simulated.
32 devices in a mesh: row: 2 (over x), col: 16 (over z, y, core).
Axes of the slice: x: 2, y: 2, z: 4, core: 2. Of those that a mesh axis runs over, the one named last changes fastest.
Arguments:
- features: bfloat16 [8192, 256], P(('row', 'col')), may hold values from -6 to 6
- weight: bfloat16 [256, 128], replicated, may hold values from -0.375 to 0.375
- tiles: bfloat16 [2, 16, 320, 128, 128], P('row', 'col'), may hold values from -0.0625 to 0.0625
- slot_tile_row: int32 [2, 16, 320], P('row', 'col'), may hold values from 0 to 3
- tile_cols: int32 [2, 16, 320], P('row', 'col'), may hold values from 0 to 31
- live_tiles: int32 [2, 16], P('row', 'col'), may hold values from 40 to 320, as said below
- cotangent: bfloat16 [8192, 128], P(('row', 'col')), may hold values from -6 to 6
Outputs:
- logits: bfloat16 [8192, 128], P(('row', 'col'))
- grad_features: bfloat16 [8192, 256], P(('row', 'col'))
- grad_weight: float32 [256, 128], replicated
Inputs may be any that keep to these rules, and one draw needn't show every extreme that they name: Slots of a block from live_tiles on are padding and not part of the adjacency; in every draw some block has all 320 slots live.
All inputs are finite; a program needn't handle non-finite values.
Results may differ from a plain program's by a relative error of at most 0.005.
Values may be sent and summed in bfloat16 or wider, within the bound.
A program may use at most 128 MiB of HBM per device.

v0:
```python
import math

import jax
import jax.numpy as jnp
from jax import lax
from jax.sharding import PartitionSpec as P


def per_device(features, weight, tiles, slot_tile_row, tile_cols, live_tiles, cotangent):
    tile_block = tiles[0, 0]
    slot_rows = slot_tile_row[0, 0]
    slot_cols = tile_cols[0, 0]
    live_count = live_tiles[0, 0]
    tile_extent = tile_block.shape[-1]
    slot_total = tile_block.shape[0]
    stretch_rows = features.shape[0]
    output_width = weight.shape[1]
    row_count = lax.axis_size("row")
    col_count = lax.axis_size("col")
    row_tiles = row_count * stretch_rows // tile_extent
    col_tiles = col_count * stretch_rows // tile_extent
    block_size = 64
    block_total = slot_total // block_size
    projected_group = jnp.dot(
        lax.all_gather(features, "col", axis=0, tiled=True),
        weight,
        preferred_element_type=jnp.float32,
    ).astype(jnp.bfloat16)
    proj_tiles = projected_group.reshape(col_tiles, tile_extent, output_width)

    def block_slice(first_slot):
        part_tiles = lax.dynamic_slice_in_dim(tile_block, first_slot, block_size, 0)
        part_rows = lax.dynamic_slice_in_dim(slot_rows, first_slot, block_size, 0)
        part_cols = lax.dynamic_slice_in_dim(slot_cols, first_slot, block_size, 0)
        live_mask = first_slot + jnp.arange(block_size, dtype=jnp.int32) < live_count
        return (part_tiles, part_rows, part_cols, live_mask)

    def forward_block(block_index, totals):
        part_tiles, part_rows, part_cols, live_mask = block_slice(block_index * block_size)
        inputs = proj_tiles[part_cols]
        products = jnp.einsum(
            "tab,tbf->taf", part_tiles, inputs, preferred_element_type=jnp.float32
        )
        segment_ids = jnp.where(live_mask, part_rows, row_tiles)
        summed = jax.ops.segment_sum(products, segment_ids, num_segments=row_tiles + 1)
        return totals + summed[:row_tiles]

    forward_totals = lax.fori_loop(
        0,
        block_total,
        forward_block,
        jnp.zeros((row_tiles, tile_extent, output_width), jnp.float32),
    )
    logits = lax.psum_scatter(
        forward_totals.reshape(row_tiles * tile_extent, output_width),
        "row",
        scatter_dimension=0,
        tiled=True,
    ).astype(jnp.bfloat16)
    cot_group = lax.all_gather(cotangent, "row", axis=0, tiled=True)
    cot_tiles = cot_group.reshape(row_tiles, tile_extent, output_width)

    def backward_block(block_index, totals):
        part_tiles, part_rows, part_cols, live_mask = block_slice(block_index * block_size)
        inputs = cot_tiles[part_rows]
        products = jnp.einsum(
            "tab,taf->tbf", part_tiles, inputs, preferred_element_type=jnp.float32
        )
        inside = live_mask & (part_cols >= 0) & (part_cols < col_tiles)
        segment_ids = jnp.where(inside, part_cols, col_tiles)
        summed = jax.ops.segment_sum(products, segment_ids, num_segments=col_tiles + 1)
        return totals + summed[:col_tiles]

    empty = jnp.zeros((col_tiles, tile_extent, output_width), jnp.float32)
    backward_totals = lax.fori_loop(0, block_total, backward_block, empty).reshape(
        col_tiles * tile_extent, output_width
    )
    back = lax.psum_scatter(backward_totals, "col", scatter_dimension=0, tiled=True)
    back_rounded = back.astype(jnp.bfloat16)
    grad_features = jnp.dot(back_rounded, weight.T, preferred_element_type=jnp.float32).astype(
        jnp.bfloat16
    )
    weight_term = lax.dot_general(
        features, back_rounded, (((0,), (0,)), ((), ())), preferred_element_type=jnp.float32
    )
    node_total = stretch_rows * row_count * col_count
    grad_weight = lax.psum(weight_term, ("row", "col")) / math.sqrt(node_total)
    return (logits, grad_features, grad_weight)


def solution(mesh):
    placed = (
        P(("row", "col"), None),
        P(),
        P("row", "col", None, None, None),
        P("row", "col", None),
        P("row", "col", None),
        P("row", "col"),
        P(("row", "col"), None),
    )
    return jax.shard_map(
        per_device,
        mesh=mesh,
        in_specs=placed,
        out_specs=(P(("row", "col"), None), P(("row", "col"), None), P()),
        check_vma=False,
    )
```

profile of v0, /device:TPU:0, one launch (start us, length us, event | category | flops | bytes accessed | tf_op | source)
XLA Modules:
  0.0 375.8 jit_solution(15768739046971264460)
XLA Ops:
  8.6 14.4 %copy.10 = bf16[1,1,320,128,128]{3,4,2,1,0:T(8,128)(2,1)} copy(bf16[1,1,320,128,128]{4,3,2,1,0:T(8,128)(2,1)} %param.13) | data formatting | bytes 20971520 | tf_op args[2]
  23.0 5.9 %all_gather.7 = bf16[512,128]{1,0:T(8,128)(2,1)S(1)} all-gather(bf16[256,128]{1,0:T(8,128)(2,1)S(1)} %copy-done.3), channel_id=1, replica_groups=mesh['row'=2,'col'=16] {'row'}, dimensions={0}, use_global_device_ids=true | all-gather | bytes 196608 | tf_op jit(solution)/shard_map/all_gather | solution.py:60
  28.9 90.2 %while.29 = (s32[]{:T(128)}, f32[32,128,128]{2,1,0:T(8,128)}, s32[]{:T(128)}, s32[320]{0:T(512)S(1)}, bf16[320,128,128]{1,2,0:T(8,128)(2,1)}, /*index=5*/s32[320...) while((s32[]{:T(128)}, f32[32,128,128]{2,1,0:T(8,128)}, ...), condition=%wide.region_6.7_spmd.clone, body=%wide.region_4.6_spmd.clone.sunk | while | flops 270534272 | bytes 33626048 | solution.py:75
  30.6 4.4 %fusion.25 = f32[64,128,128]{2,1,0:T(8,128)} fusion(bf16[64,128,128]{2,1,0:T(8,128)(2,1)S(1)} %gather_fusion.1, bf16[320,128,128]{1,2,0:T(8,128)(2,1)} %get-tuple-element.501, s32[]{:T(128)S(6)} %select_n.64), kind=kOutput, calls=%fused_computation.12.clone.1 | convolution fusion | flops 268435456 | bytes 8388612 | tf_op jit(solution)/shard_map/while/body/eval_jaxpr/tab,taf->tbf/dot_general | solution.py:66
  35.2 8.8 %scatter_fusion.1 = f32[33,128,128]{2,1,0:T(8,128)S(1)} fusion(f32[33,128,128]{2,1,0:T(8,128)S(1)} %broadcast.112, s32[64]{0:T(128)S(1)} %get-tuple-element.435, f32[64,128,128]{2,1,0:T(8,128)} %fusion.25), kind=kCustom, calls=%fused_computation.3.clone.clone.1 | custom fusion | flops 1048576 | bytes 12583168 | tf_op jit(solution)/shard_map/while/body/eval_jaxpr/scatter-add | solution.py:71
  47.4 4.4 %fusion.25 = f32[64,128,128]{2,1,0:T(8,128)} fusion(bf16[64,128,128]{2,1,0:T(8,128)(2,1)S(1)} %gather_fusion.1, bf16[320,128,128]{1,2,0:T(8,128)(2,1)} %get-tuple-element.501, s32[]{:T(128)S(6)} %select_n.64), kind=kOutput, calls=%fused_computation.12.clone.1 | convolution fusion | flops 268435456 | bytes 8388612 | tf_op jit(solution)/shard_map/while/body/eval_jaxpr/tab,taf->tbf/dot_general | solution.py:66
  52.0 8.8 %scatter_fusion.1 = f32[33,128,128]{2,1,0:T(8,128)S(1)} fusion(f32[33,128,128]{2,1,0:T(8,128)S(1)} %broadcast.112, s32[64]{0:T(128)S(1)} %get-tuple-element.435, f32[64,128,128]{2,1,0:T(8,128)} %fusion.25), kind=kCustom, calls=%fused_computation.3.clone.clone.1 | custom fusion | flops 1048576 | bytes 12583168 | tf_op jit(solution)/shard_map/while/body/eval_jaxpr/scatter-add | solution.py:71
  65.7 4.4 %fusion.25 = f32[64,128,128]{2,1,0:T(8,128)} fusion(bf16[64,128,128]{2,1,0:T(8,128)(2,1)S(1)} %gather_fusion.1, bf16[320,128,128]{1,2,0:T(8,128)(2,1)} %get-tuple-element.501, s32[]{:T(128)S(6)} %select_n.64), kind=kOutput, calls=%fused_computation.12.clone.1 | convolution fusion | flops 268435456 | bytes 8388612 | tf_op jit(solution)/shard_map/while/body/eval_jaxpr/tab,taf->tbf/dot_general | solution.py:66
  70.3 8.8 %scatter_fusion.1 = f32[33,128,128]{2,1,0:T(8,128)S(1)} fusion(f32[33,128,128]{2,1,0:T(8,128)S(1)} %broadcast.112, s32[64]{0:T(128)S(1)} %get-tuple-element.435, f32[64,128,128]{2,1,0:T(8,128)} %fusion.25), kind=kCustom, calls=%fused_computation.3.clone.clone.1 | custom fusion | flops 1048576 | bytes 12583168 | tf_op jit(solution)/shard_map/while/body/eval_jaxpr/scatter-add | solution.py:71
  84.1 4.4 %fusion.25 = f32[64,128,128]{2,1,0:T(8,128)} fusion(bf16[64,128,128]{2,1,0:T(8,128)(2,1)S(1)} %gather_fusion.1, bf16[320,128,128]{1,2,0:T(8,128)(2,1)} %get-tuple-element.501, s32[]{:T(128)S(6)} %select_n.64), kind=kOutput, calls=%fused_computation.12.clone.1 | convolution fusion | flops 268435456 | bytes 8388612 | tf_op jit(solution)/shard_map/while/body/eval_jaxpr/tab,taf->tbf/dot_general | solution.py:66
  88.7 8.8 %scatter_fusion.1 = f32[33,128,128]{2,1,0:T(8,128)S(1)} fusion(f32[33,128,128]{2,1,0:T(8,128)S(1)} %broadcast.112, s32[64]{0:T(128)S(1)} %get-tuple-element.435, f32[64,128,128]{2,1,0:T(8,128)} %fusion.25), kind=kCustom, calls=%fused_computation.3.clone.clone.1 | custom fusion | flops 1048576 | bytes 12583168 | tf_op jit(solution)/shard_map/while/body/eval_jaxpr/scatter-add | solution.py:71
  102.4 4.4 %fusion.25 = f32[64,128,128]{2,1,0:T(8,128)} fusion(bf16[64,128,128]{2,1,0:T(8,128)(2,1)S(1)} %gather_fusion.1, bf16[320,128,128]{1,2,0:T(8,128)(2,1)} %get-tuple-element.501, s32[]{:T(128)S(6)} %select_n.64), kind=kOutput, calls=%fused_computation.12.clone.1 | convolution fusion | flops 268435456 | bytes 8388612 | tf_op jit(solution)/shard_map/while/body/eval_jaxpr/tab,taf->tbf/dot_general | solution.py:66
  107.1 8.8 %scatter_fusion.1 = f32[33,128,128]{2,1,0:T(8,128)S(1)} fusion(f32[33,128,128]{2,1,0:T(8,128)S(1)} %broadcast.112, s32[64]{0:T(128)S(1)} %get-tuple-element.435, f32[64,128,128]{2,1,0:T(8,128)} %fusion.25), kind=kCustom, calls=%fused_computation.3.clone.clone.1 | custom fusion | flops 1048576 | bytes 12583168 | tf_op jit(solution)/shard_map/while/body/eval_jaxpr/scatter-add | solution.py:71
  119.9 62.9 %reduce-scatter.5.cloned.1.call-done = f32[256,128]{1,0:T(8,128)} async-done(((f32[4096,128]{1,0:T(8,128)}), f32[256,128]{1,0:T(8,128)}) %reduce-scatter.5.cloned.1.call-update) | async-done | bytes 131088 | tf_op jit(solution)/shard_map/reduce_scatter | solution.py:78
  184.7 40.8 %all-gather.2.cloned.1.call-done = bf16[4096,256]{1,0:T(8,128)(2,1)} async-done(((bf16[256,256]{1,0:T(8,128)(2,1)}), bf16[4096,256]{1,0:T(8,128)(2,1)}) %all-gather.2.cloned.1.call-update) | async-done | bytes 2097168 | tf_op jit(solution)/shard_map/all_gather | solution.py:25
  227.7 74.2 %while.28 = (s32[]{:T(128)}, f32[4,128,128]{2,1,0:T(8,128)S(1)}, s32[]{:T(128)}, s32[320]{0:T(512)S(1)}, bf16[320,128,128]{2,1,0:T(8,128)(2,1)}, /*index=5*/s32[...) while((s32[]{:T(128)}, f32[4,128,128]{2,1,0:T(8,128)S(1)}, ...), condition=%wide.region_2.3_spmd.clone, body=%wide.region_0.2_spmd.clone.sunk | while | flops 269616512 | bytes 26286016 | solution.py:48
  233.7 8.8 %scatter_fusion = f32[5,128,128]{2,1,0:T(8,128)S(1)} fusion(f32[5,128,128]{2,1,0:T(8,128)S(1)} %broadcast.105, s32[64]{0:T(128)S(1)} %get-tuple-element.426, f32[64,128,128]{2,1,0:T(8,128)} %fusion.22), kind=kCustom, calls=%fused_computation.2.clone.clone.1 | custom fusion | flops 1048576 | bytes 12583168 | tf_op jit(solution)/shard_map/while/body/eval_jaxpr/scatter-add | solution.py:45
  248.5 8.8 %scatter_fusion = f32[5,128,128]{2,1,0:T(8,128)S(1)} fusion(f32[5,128,128]{2,1,0:T(8,128)S(1)} %broadcast.105, s32[64]{0:T(128)S(1)} %get-tuple-element.426, f32[64,128,128]{2,1,0:T(8,128)} %fusion.22), kind=kCustom, calls=%fused_computation.2.clone.clone.1 | custom fusion | flops 1048576 | bytes 12583168 | tf_op jit(solution)/shard_map/while/body/eval_jaxpr/scatter-add | solution.py:45
  263.4 8.8 %scatter_fusion = f32[5,128,128]{2,1,0:T(8,128)S(1)} fusion(f32[5,128,128]{2,1,0:T(8,128)S(1)} %broadcast.105, s32[64]{0:T(128)S(1)} %get-tuple-element.426, f32[64,128,128]{2,1,0:T(8,128)} %fusion.22), kind=kCustom, calls=%fused_computation.2.clone.clone.1 | custom fusion | flops 1048576 | bytes 12583168 | tf_op jit(solution)/shard_map/while/body/eval_jaxpr/scatter-add | solution.py:45
  278.3 8.8 %scatter_fusion = f32[5,128,128]{2,1,0:T(8,128)S(1)} fusion(f32[5,128,128]{2,1,0:T(8,128)S(1)} %broadcast.105, s32[64]{0:T(128)S(1)} %get-tuple-element.426, f32[64,128,128]{2,1,0:T(8,128)} %fusion.22), kind=kCustom, calls=%fused_computation.2.clone.clone.1 | custom fusion | flops 1048576 | bytes 12583168 | tf_op jit(solution)/shard_map/while/body/eval_jaxpr/scatter-add | solution.py:45
  288.8 4.2 %fusion.22 = f32[64,128,128]{2,1,0:T(8,128)} fusion(bf16[64,128,128]{2,1,0:T(8,128)(2,1)S(1)} %gather_fusion, bf16[320,128,128]{2,1,0:T(8,128)(2,1)} %get-tuple-element.465, s32[]{:T(128)S(6)} %select_n.62), kind=kOutput, calls=%fused_computation.4.clone.1 | convolution fusion | flops 268435456 | bytes 8388612 | tf_op jit(solution)/shard_map/while/body/eval_jaxpr/tab,tbf->taf/dot_general | solution.py:41
  293.1 8.8 %scatter_fusion = f32[5,128,128]{2,1,0:T(8,128)S(1)} fusion(f32[5,128,128]{2,1,0:T(8,128)S(1)} %broadcast.105, s32[64]{0:T(128)S(1)} %get-tuple-element.426, f32[64,128,128]{2,1,0:T(8,128)} %fusion.22), kind=kCustom, calls=%fused_computation.2.clone.clone.1 | custom fusion | flops 1048576 | bytes 12583168 | tf_op jit(solution)/shard_map/while/body/eval_jaxpr/scatter-add | solution.py:45
  304.5 50.3 %all-reduce.2.cloned.1.call-done = f32[256,128]{0,1:T(8,128)} async-done(((f32[256,128]{0,1:T(8,128)}), f32[256,128]{0,1:T(8,128)}) %all-reduce.2.cloned.1.call-update) | async-done | bytes 131088 | tf_op jit(solution)/shard_map/psum | solution.py:87
  356.5 11.2 %reduce-scatter.3.cloned.1.call-done = f32[256,128]{1,0:T(8,128)} async-done(((f32[512,128]{1,0:T(8,128)}), f32[256,128]{1,0:T(8,128)}) %reduce-scatter.3.cloned.1.call-update) | async-done | bytes 131088 | tf_op jit(solution)/shard_map/reduce_scatter | solution.py:54
  (80 shorter events, 62.0 us)
Async XLA Ops:
  7.2 218.3 %copy-start = (bf16[256,128]{1,0:T(8,128)(2,1)S(1)}, bf16[256,128]{1,0:T(8,128)(2,1)}, u32[]{:S(2)}) copy-start(bf16[256,128]{1,0:T(8,128)(2,1)} %param.12) | copy-start | bytes 196612
  7.2 175.7 %reduce-scatter.5.cloned.1.call-start = ((), (), s32[]{:S(2)}) async-start(), calls=%async_computation.4 | async-start | bytes 2228224 | tf_op jit(solution)/shard_map/reduce_scatter | solution.py:78
  8.6 14.4 %copy-start.3 = (bf16[256,128]{1,0:T(8,128)(2,1)S(1)}, bf16[256,128]{1,0:T(8,128)(2,1)}, u32[]{:S(2)}) copy-start(bf16[256,128]{1,0:T(8,128)(2,1)} %param.17) | copy-start | bytes 196612
  119.1 63.7 %copy-start.2 = (bf16[256,256]{1,0:T(8,128)(2,1)S(1)}, bf16[256,256]{1,0:T(8,128)(2,1)}, u32[]{:S(2)}) copy-start(bf16[256,256]{1,0:T(8,128)(2,1)} %param.11) | copy-start | bytes 393220
  119.1 106.3 %all-gather.2.cloned.1.call-start = ((), (), s32[]{:S(2)}) async-start(), calls=%async_computation.2 | async-start | bytes 2228224 | tf_op jit(solution)/shard_map/all_gather | solution.py:25
  119.9 234.9 %all-reduce.2.cloned.1.call-start = ((), (), s32[]{:S(2)}) async-start(), calls=%async_computation.5 | async-start | bytes 262144 | tf_op jit(solution)/shard_map/psum | solution.py:87
  184.6 183.1 %reduce-scatter.3.cloned.1.call-start = ((), (), s32[]{:S(2)}) async-start(), calls=%async_computation.3 | async-start | bytes 393216 | tf_op jit(solution)/shard_map/reduce_scatter | solution.py:54
  302.0 0.7 copy-start.1
Sparse Core Ops, SparseCore 0:
  119.3 63.5 reduce-scatter.4
  185.0 40.3 all-gather.1
  231.6 123.1 all-reduce.1
  356.9 10.7 reduce-scatter.2
where the time goes:
time: 378 us; the launch traced here: 376 us
  waiting for transfers between devices  166 us (44%)
  other arithmetic  114 us (30%)
  matrix products  48.8 us (13%)
  local copies, waits for them, and re-layouts  26.7 us (7%)
  between operations  13.8 us (4%)
  blocking collectives  5.85 us (2%)
    reduce_scatter x1, waiting for transfers between devices, per_device(): lax.psum_scatter(backward_totals, 'col', scatter_dimension=0, tiled=True)  62.9 us
    psum x1, waiting for transfers between devices, per_device(): grad_weight = lax.psum(weight_term, ('row', 'col')) / math.sqrt(node_total)  50.3 us
    scatter-add x5, other arithmetic, backward_block(): jax.ops.segment_sum(products, segment_ids, num_segments=col_tiles + 1)  44 us
    scatter-add x5, other arithmetic, forward_block(): jax.ops.segment_sum(products, segment_ids, num_segments=row_tiles + 1)  43.9 us
    all_gather x1, waiting for transfers between devices, per_device(): lax.all_gather(features, 'col', axis=0, tiled=True)  40.8 us
    dot_general x5, matrix products, backward_block(): jnp.einsum('tab,taf->tbf', part_tiles, inputs, preferred_element_type=jnp...  21.9 us
    dot_general x5, matrix products, forward_block(): jnp.einsum('tab,tbf->taf', part_tiles, inputs, preferred_element_type=jnp...  21.1 us
    unnamed x10, local copies, waits for them, and re-layouts  15.9 us
  transfers between devices with their start and end apart: 4, of which 4 were waited for; matrix products, arithmetic and copies ran while one was open for 22% of the time, Pallas kernels for 0%

commit v1 on v0

v1 whole, which is shorter than its diff:
```python
import functools
import math

import jax
import jax.numpy as jnp
from jax import lax
from jax.experimental import pallas as pl
from jax.experimental.pallas import tpu as pltpu
from jax.sharding import PartitionSpec as P

MESH = pl.DeviceIdType.MESH
F32 = jnp.float32
BF16 = jnp.bfloat16


def kernel(dims, features, weight, tiles, slot_rows, slot_cols, live, cot,
           logits, grad_features, grad_weight,
           tile_buf, sums, proj, cots, cots_t, feat_t, code_v, last_v, code, last,
           sib_out, sib_in, y_out, y_in, z_out, z_in, log_out, log_in,
           term_out, term_in, total,
           tile_sem, smem_sem, cot_send, cot_recv, ag_send, ag_recv,
           sib_send, sib_recv, y_send, y_recv, z_send, z_recv,
           log_send, log_recv, term_send, term_recv, tot_send, tot_recv):
    R, C, O, I = dims
    n = R * C
    slots = tiles.shape[0]
    side = tiles.shape[1]
    stretch = features.shape[0]
    per = stretch // side
    col_tiles = C * per
    cells = R * per * col_tiles
    r, c = lax.axis_index("row"), lax.axis_index("col")
    me = r * C + c
    k = lax.rem(c, 2)
    q = c // 2
    y = lax.rem(q, I)
    z = q // I

    def col_of(zz, yy, kk):
        return (zz * I + yy) * 2 + kk

    def remote(src, dst, send, recv, dev):
        return pltpu.make_async_remote_copy(
            src_ref=src, dst_ref=dst, send_sem=send, recv_sem=recv,
            device_id=dev, device_id_type=MESH)

    chunks = tile_sem.shape[0]
    chunk = slots // chunks
    loads = [
        pltpu.make_async_copy(tiles.at[pl.ds(i * chunk, chunk)],
                              tile_buf.at[pl.ds(i * chunk, chunk)], tile_sem.at[i])
        for i in range(chunks)
    ]
    for load in loads:
        load.start()

    barrier = pltpu.get_barrier_semaphore()

    def greet(d, carry):
        t = lax.rem(me + d, n)
        pl.semaphore_signal(barrier, inc=1, device_id=(t // C, lax.rem(t, C)), device_id_type=MESH)
        return carry

    lax.fori_loop(1, n, greet, 0)
    proj[c] = jnp.dot(features[...], weight[...], preferred_element_type=F32).astype(BF16)
    pl.semaphore_wait(barrier, n - 1)

    pending = []

    def gather_send(block, dev):
        copy = remote(proj.at[block], proj.at[block], ag_send.at[len(pending)],
                      ag_recv.at[block], (r, dev))
        copy.start()
        pending.append(copy)

    def gather_wait(block):
        remote(proj.at[block], proj.at[block], ag_send.at[0], ag_recv.at[block],
               (r, c)).wait_recv()

    cot_copies = []
    for d in range(1, R):
        peer = lax.rem(r + d, R)
        copy = remote(cot, cots.at[r], cot_send.at[d], cot_recv.at[r], (peer, c))
        copy.start()
        cot_copies.append(copy)
    z_peers = [lax.rem(z + d, O) for d in range(1, O)]
    y_peers = [lax.rem(y + d, I) for d in range(1, I)]
    for yy in y_peers:
        gather_send(c, col_of(z, yy, k))
    for zz in z_peers:
        gather_send(c, col_of(zz, y, k))
    gather_send(c, col_of(z, y, 1 - k))

    lane = lax.broadcasted_iota(jnp.int32, (1, slots), 1)
    cell = jnp.where(lane < live[0, 0], slot_rows[...] * col_tiles + slot_cols[...], cells)
    eye = (lax.broadcasted_iota(jnp.int32, (slots, slots), 0)
           == lax.broadcasted_iota(jnp.int32, (slots, slots), 1))
    cell_c = jnp.sum(jnp.where(eye, cell, 0), axis=1, keepdims=True)
    sub = lax.broadcasted_iota(jnp.int32, (slots, 1), 0)
    same_before = (cell == cell_c) & (lane < sub)
    rank = jnp.sum(((cell < cell_c) | same_before).astype(jnp.int32), axis=1, keepdims=True)
    keep = jnp.max(same_before.astype(jnp.int32), axis=1, keepdims=True)
    code_v[...] = jnp.sum(jnp.where(rank == lane, sub * 2 + keep, 0), axis=0, keepdims=True)
    cell_ids = lax.broadcasted_iota(jnp.int32, (1, cells), 1)
    upto = jnp.sum((cell_c <= cell_ids).astype(jnp.int32), axis=0, keepdims=True)
    held = jnp.max((cell_c == cell_ids).astype(jnp.int32), axis=0, keepdims=True)
    last_v[...] = upto * held
    to_smem = [pltpu.make_async_copy(code_v, code, smem_sem.at[0]),
               pltpu.make_async_copy(last_v, last, smem_sem.at[1])]
    for copy in to_smem:
        copy.start()
    feat_t[...] = features[...].astype(F32).T.astype(BF16)
    cots_t[r] = cot[...].astype(F32).T.astype(BF16)
    sums[0] = jnp.zeros((side, side), BF16)
    for copy in to_smem:
        copy.wait()
    for load in loads:
        load.wait()

    def add_slot(j, acc):
        word = code[0, j]
        keep_it = lax.rem(word, 2).astype(F32)
        acc = acc * keep_it + tile_buf[word // 2].astype(F32)
        sums[j + 1] = acc.astype(BF16)
        return acc

    parts = 4
    acc = jnp.zeros((side, side), F32)
    for part in range(parts):
        acc = lax.fori_loop(part * slots // parts, (part + 1) * slots // parts, add_slot, acc,
                            unroll=2)
        if part == 1:
            for zz in z_peers:
                block = col_of(zz, y, k)
                gather_wait(block)
                for yy in y_peers:
                    gather_send(block, col_of(z, yy, k))
                gather_send(block, col_of(z, y, 1 - k))
        if part == parts - 1:
            for d in range(O):
                zz = lax.rem(z + d, O)
                for yy in y_peers:
                    block = col_of(zz, yy, k)
                    gather_wait(block)
                    gather_send(block, col_of(z, y, 1 - k))

    for d in range(1, R):
        peer = lax.rem(r + d, R)
        remote(cot, cots.at[peer], cot_send.at[d], cot_recv.at[peer], (peer, c)).wait_recv()
        cots_t[peer] = cots[peer].astype(F32).T.astype(BF16)

    def stretch_block(s, b):
        rows = []
        for a in range(per):
            base = (s * per + a) * col_tiles + b * per
            rows.append(jnp.concatenate([sums[last[0, base + e]] for e in range(per)], axis=1))
        return jnp.concatenate(rows, axis=0)

    def back_block(b):
        out = jnp.dot(cots_t[0], stretch_block(0, b), preferred_element_type=F32)
        for s in range(1, R):
            out = out + jnp.dot(cots_t[s], stretch_block(s, b), preferred_element_type=F32)
        return out

    def place(i):
        zz = lax.rem(z + lax.rem(i, O) + 1, O)
        yy = lax.rem(y + i // O + 1, I)
        return zz, yy

    def sib_copy(m):
        return remote(sib_out.at[m], sib_in.at[m], sib_send.at[m], sib_recv.at[m],
                      (r, col_of(z, y, 1 - k)))

    def send_sib(i, carry):
        zz, yy = place(i)
        m = zz * I + yy
        sib_out[m] = back_block(2 * m + 1 - k).astype(BF16)
        sib_copy(m).start()
        return carry

    lax.fori_loop(0, O * I, send_sib, 0)

    def y_copy(zz, yy):
        return remote(y_out.at[zz * I + yy], y_in.at[y * O + zz], y_send.at[zz * I + yy],
                      y_recv.at[y * O + zz], (r, col_of(z, yy, k)))

    def send_y(i, carry):
        zz, yy = place(i)
        m = zz * I + yy
        mine = back_block(2 * m + k)
        sib_copy(m).wait_recv()
        y_out[m] = (mine + sib_in[m].astype(F32)).astype(BF16)
        y_copy(zz, yy).start()
        return carry

    lax.fori_loop(0, O * (I - 1), send_y, 0)

    for d in range(O):
        for e in range(I):
            gather_wait(col_of(lax.rem(z + d, O), lax.rem(y + e, I), 1 - k))
    group = 4 if C % 4 == 0 else 1

    def forward(s):
        def step(g, out):
            for b in range(group):
                out = out + jnp.dot(stretch_block(s, g * group + b), proj[g * group + b],
                                    preferred_element_type=F32)
            return out
        return lax.fori_loop(0, C // group, step, jnp.zeros((stretch, proj.shape[2]), F32))

    log_copies = []
    for d in range(1, R):
        peer = lax.rem(r + d, R)
        log_out[d - 1] = forward(peer)
        copy = remote(log_out.at[d - 1], log_in.at[r], log_send.at[d], log_recv.at[r], (peer, c))
        copy.start()
        log_copies.append(copy)
    mine_log = forward(r)

    def summed(zz):
        m = zz * I + y
        value = back_block(2 * m + k)
        sib_copy(m).wait_recv()
        value = value + sib_in[m].astype(F32)
        for yy in y_peers:
            slot = yy * O + zz
            remote(y_out.at[0], y_in.at[slot], y_send.at[0], y_recv.at[slot],
                   (r, c)).wait_recv()
            value = value + y_in[slot].astype(F32)
        return value

    z_copies = []
    for d in range(1, O):
        zz = lax.rem(z + d, O)
        z_out[d - 1] = summed(zz).astype(BF16)
        copy = remote(z_out.at[d - 1], z_in.at[z], z_send.at[d - 1], z_recv.at[z],
                      (r, col_of(zz, y, k)))
        copy.start()
        z_copies.append(copy)
    back_t = summed(z)
    for d in range(1, R):
        peer = lax.rem(r + d, R)
        remote(log_out.at[0], log_in.at[peer], log_send.at[0], log_recv.at[peer],
               (peer, c)).wait_recv()
        mine_log = mine_log + log_in[peer]
    logits[...] = mine_log.astype(BF16)
    for zz in z_peers:
        remote(z_out.at[0], z_in.at[zz], z_send.at[0], z_recv.at[zz], (r, c)).wait_recv()
        back_t = back_t + z_in[zz].astype(F32)
    back = back_t.T.astype(BF16)
    term = jnp.dot(feat_t[...], back, preferred_element_type=F32)

    owners = term_out.shape[0]
    rows = term_out.shape[1]
    term_out[...] = term.reshape(term_out.shape)

    def term_copy(t):
        return remote(term_out.at[t], term_in.at[me], term_send.at[t], term_recv.at[me],
                      (t // C, lax.rem(t, C)))

    def term_arrival(t):
        return remote(term_out.at[0], term_in.at[t], term_send.at[0], term_recv.at[t], (r, c))

    def tot_copy(t):
        return remote(total.at[me], total.at[me], tot_send.at[t], tot_recv.at[me],
                      (t // C, lax.rem(t, C)))

    def tot_arrival(t):
        return remote(total.at[t], total.at[t], tot_send.at[0], tot_recv.at[t], (r, c))

    def others(count, act):
        def body(d, carry):
            t = lax.rem(me + d, n)
            if count == n:
                act(t)
            else:
                @pl.when(t < count)
                def _():
                    act(t)
            return carry
        lax.fori_loop(1, n, body, 0)

    def own_part():
        term_in[me] = term_out[me]
        others(n, lambda t: term_arrival(t).wait_recv())
        total[me] = jnp.sum(term_in[...], axis=0) * (1.0 / math.sqrt(n * stretch))
        others(n, lambda t: tot_copy(t).start())

    others(owners, lambda t: term_copy(t).start())
    grad_features[...] = lax.dot_general(
        back, weight[...], (((1,), (1,)), ((), ())), preferred_element_type=F32).astype(BF16)
    if owners == n:
        own_part()
    else:
        pl.when(me < owners)(own_part)
    for copy in pending + cot_copies + log_copies + z_copies:
        copy.wait_send()

    def drain_sib(m, carry):
        sib_copy(m).wait_send()
        return carry

    lax.fori_loop(0, O * I, drain_sib, 0)

    def drain_y(i, carry):
        zz, yy = place(i)
        y_copy(zz, yy).wait_send()
        return carry

    lax.fori_loop(0, O * (I - 1), drain_y, 0)
    others(owners, lambda t: term_copy(t).wait_send())
    others(owners, lambda t: tot_arrival(t).wait_recv())
    grad_weight[...] = total[...].reshape(grad_weight.shape)
    if owners == n:
        others(n, lambda t: tot_copy(t).wait_send())
    else:
        @pl.when(me < owners)
        def _():
            others(n, lambda t: tot_copy(t).wait_send())


def per_device(R, C, features, weight, tiles, slot_tile_row, tile_cols, live_tiles, cotangent):
    slots, side = tiles.shape[2], tiles.shape[3]
    stretch, width = features.shape
    out_width = weight.shape[1]
    half = C // 2
    O = 4 if half % 4 == 0 else half
    I = half // O
    n = R * C
    per = stretch // side
    cells = R * per * C * per
    owners = min(n, width // 8)
    rows = width // owners
    chunks = 8 if slots % 8 == 0 else 1
    dma = pltpu.SemaphoreType.DMA
    vmem = pltpu.VMEM
    blk = (out_width, stretch)
    gathers = (O - 1) + (I - 1) + 1 + (O - 1) * I + O * (I - 1)
    scratch = [
        vmem((slots, side, side), BF16),
        vmem((slots + 1, side, side), BF16),
        vmem((C, stretch, out_width), BF16),
        vmem((R, stretch, out_width), BF16),
        vmem((R,) + blk, BF16),
        vmem((width, stretch), BF16),
        vmem((1, slots), jnp.int32),
        vmem((1, cells), jnp.int32),
        pltpu.SMEM((1, slots), jnp.int32),
        pltpu.SMEM((1, cells), jnp.int32),
        vmem((half,) + blk, BF16),
        vmem((half,) + blk, BF16),
        vmem((half,) + blk, BF16),
        vmem((half,) + blk, BF16),
        vmem((max(O - 1, 1),) + blk, BF16),
        vmem((O,) + blk, BF16),
        vmem((max(R - 1, 1), stretch, out_width), F32),
        vmem((R, stretch, out_width), F32),
        vmem((owners, rows, out_width), F32),
        vmem((n, rows, out_width), F32),
        vmem((owners, rows, out_width), F32),
        dma((chunks,)), dma((2,)), dma((R,)), dma((R,)),
        dma((gathers,)), dma((C,)),
        dma((half,)), dma((half,)), dma((half,)), dma((half,)),
        dma((O,)), dma((O,)), dma((R,)), dma((R,)),
        dma((n,)), dma((n,)), dma((n,)), dma((n,)),
    ]
    v = pl.BlockSpec(memory_space=pltpu.VMEM)
    return pl.pallas_call(
        functools.partial(kernel, (R, C, O, I)),
        out_shape=(
            jax.ShapeDtypeStruct((stretch, out_width), BF16),
            jax.ShapeDtypeStruct((stretch, width), BF16),
            jax.ShapeDtypeStruct((width, out_width), F32),
        ),
        in_specs=[v, v, pl.BlockSpec(memory_space=pl.ANY), v, v,
                  pl.BlockSpec(memory_space=pltpu.SMEM), v],
        out_specs=(v, v, v),
        scratch_shapes=scratch,
        compiler_params=pltpu.CompilerParams(
            collective_id=0, has_side_effects=True, vmem_limit_bytes=60 * 1024 * 1024),
    )(features, weight, tiles.reshape(slots, side, side), slot_tile_row.reshape(1, slots),
      tile_cols.reshape(1, slots), live_tiles, cotangent)


def solution(mesh):
    R, C = mesh.shape["row"], mesh.shape["col"]
    placed = (
        P(("row", "col"), None),
        P(),
        P("row", "col", None, None, None),
        P("row", "col", None),
        P("row", "col", None),
        P("row", "col"),
        P(("row", "col"), None),
    )
    return jax.shard_map(
        functools.partial(per_device, R, C),
        mesh=mesh,
        in_specs=placed,
        out_specs=(P(("row", "col"), None), P(("row", "col"), None), P()),
        check_vma=False,
    )
```

time: 378 us -> 53.3 us (0.14)
  waiting for transfers between devices: 166 us -> 0 us
  other arithmetic: 114 us -> 0 us
  matrix products: 48.8 us -> 0 us
  Pallas kernels: 0 us -> 47.1 us
  local copies, waits for them, and re-layouts: 26.7 us -> 4.61 us
  between operations: 13.8 us -> 1.29 us
  blocking collectives: 5.85 us -> 0 us
    scatter-add x10 -> x0, other arithmetic: 87.9 us -> none  [the longest x5 44 us: backward_block(): jax.ops.segment_sum(products, segment_ids, num_segments=col_tiles + 1)]
    reduce_scatter x2 -> x0, waiting for transfers between devices: 74.1 us -> none  [the longest x1 62.9 us: per_device(): lax.psum_scatter(backward_totals, 'col', scatter_dimension=0, tiled=True)]
    psum x1 -> x0, waiting for transfers between devices: 50.3 us -> none  [per_device(): grad_weight = lax.psum(weight_term, ('row', 'col')) / math.sqrt(node_total)]
    dot_general x13 -> x0, matrix products: 48.8 us -> none  [the longest x5 21.9 us: backward_block(): jnp.einsum('tab,taf->tbf', part_tiles, inputs, preferred_element_type=jnp...]
    pallas_call x0 -> x1, Pallas kernels: none -> 47.1 us  [per_device(): pl.pallas_call(functools.partial(kernel, (R, C, O, I)), out_shape=(jax.Sh...]
    all_gather x1 -> x0, waiting for transfers between devices: 40.8 us -> none  [per_device(): lax.all_gather(features, 'col', axis=0, tiled=True)]
    add x10 -> x0, other arithmetic: 14.9 us -> none  [the longest x5 14.6 us: backward_block(): return totals + summed[:col_tiles]]
    unnamed x10 -> x3, local copies, waits for them, and re-layouts: 15.9 us -> 4.61 us
  transfers between devices with their start and end apart: 4 -> 0, of which waited for: 4 -> 0; matrix products, arithmetic and copies ran while one was open for 22% -> 0% of each run, Pallas kernels for 0% -> 0%
where the time goes in v1:
time: 53.3 us; the launch traced here: 53 us
  Pallas kernels  47.1 us (88%)
  local copies, waits for them, and re-layouts  4.61 us (9%)
  between operations  1.29 us (2%)
    pallas_call x1, Pallas kernels, per_device(): pl.pallas_call(functools.partial(kernel, (R, C, O, I)), out_shape=(jax.Sh...  47.1 us
    unnamed x3, local copies, waits for them, and re-layouts  4.61 us

profile of v1, /device:TPU:0, one launch (start us, length us, event | category | flops | bytes accessed | tf_op | source)
XLA Modules:
  0.0 53.0 jit_solution(15221192029488530999)
XLA Ops:
  1.3 47.1 %shard_map.94 = (bf16[256,128]{1,0:T(8,128)(2,1)}, bf16[256,256]{1,0:T(8,128)(2,1)}, f32[256,128]{1,0:T(8,128)}) custom-call(bf16[256,256]{1,0:T(8,128)(2,1)} %features.1, bf16[256,128]{1,0:T(8,128)(2,1)} %weight.1, bf16[320,128,128]{2,1,0:T(8,128)(2,1)} %bitcast.3, s32[1,320]{1,0:T(1,128)} %bitcast.4, s32[1,320]{1,0:T(1,128)} %bitcast.5, ...), custom_call_target="tpu_custom_call" | custom-call | tf_op jit(solution)/shard_map/pallas_call | solution.py:368
  48.4 1.5 %copy.14 = bf16[256,128]{1,0:T(8,128)(2,1)} copy(bf16[256,128]{1,0:T(8,128)(2,1)} %get-tuple-element.6) | data formatting | bytes 131072
  49.9 1.6 %copy.15 = bf16[256,256]{1,0:T(8,128)(2,1)} copy(bf16[256,256]{1,0:T(8,128)(2,1)} %get-tuple-element.7) | data formatting | bytes 262144
  51.5 1.6 %copy.16 = f32[256,128]{1,0:T(8,128)} copy(f32[256,128]{1,0:T(8,128)} %get-tuple-element.8) | data formatting | bytes 262144

commit v2 on v1

--- a/solution.py
+++ b/solution.py
@@ -61,36 +61,8 @@
         pl.semaphore_signal(barrier, inc=1, device_id=(t // C, lax.rem(t, C)), device_id_type=MESH)
         return carry
 
-    lax.fori_loop(1, n, greet, 0)
+    lax.fori_loop(1, n, greet, 0, unroll=n - 1 if n <= 32 else 1)
     proj[c] = jnp.dot(features[...], weight[...], preferred_element_type=F32).astype(BF16)
-    pl.semaphore_wait(barrier, n - 1)
-
-    pending = []
-
-    def gather_send(block, dev):
-        copy = remote(proj.at[block], proj.at[block], ag_send.at[len(pending)],
-                      ag_recv.at[block], (r, dev))
-        copy.start()
-        pending.append(copy)
-
-    def gather_wait(block):
-        remote(proj.at[block], proj.at[block], ag_send.at[0], ag_recv.at[block],
-               (r, c)).wait_recv()
-
-    cot_copies = []
-    for d in range(1, R):
-        peer = lax.rem(r + d, R)
-        copy = remote(cot, cots.at[r], cot_send.at[d], cot_recv.at[r], (peer, c))
-        copy.start()
-        cot_copies.append(copy)
-    z_peers = [lax.rem(z + d, O) for d in range(1, O)]
-    y_peers = [lax.rem(y + d, I) for d in range(1, I)]
-    for yy in y_peers:
-        gather_send(c, col_of(z, yy, k))
-    for zz in z_peers:
-        gather_send(c, col_of(zz, y, k))
-    gather_send(c, col_of(z, y, 1 - k))
-
     lane = lax.broadcasted_iota(jnp.int32, (1, slots), 1)
     cell = jnp.where(lane < live[0, 0], slot_rows[...] * col_tiles + slot_cols[...], cells)
     eye = (lax.broadcasted_iota(jnp.int32, (slots, slots), 0)
@@ -112,6 +84,34 @@
     feat_t[...] = features[...].astype(F32).T.astype(BF16)
     cots_t[r] = cot[...].astype(F32).T.astype(BF16)
     sums[0] = jnp.zeros((side, side), BF16)
+    pl.semaphore_wait(barrier, n - 1)
+
+    pending = []
+
+    def gather_send(block, dev):
+        copy = remote(proj.at[block], proj.at[block], ag_send.at[len(pending)],
+                      ag_recv.at[block], (r, dev))
+        copy.start()
+        pending.append(copy)
+
+    def gather_wait(block):
+        remote(proj.at[block], proj.at[block], ag_send.at[0], ag_recv.at[block],
+               (r, c)).wait_recv()
+
+    cot_copies = []
+    for d in range(1, R):
+        peer = lax.rem(r + d, R)
+        copy = remote(cot, cots.at[r], cot_send.at[d], cot_recv.at[r], (peer, c))
+        copy.start()
+        cot_copies.append(copy)
+    z_peers = [lax.rem(z + d, O) for d in range(1, O)]
+    y_peers = [lax.rem(y + d, I) for d in range(1, I)]
+    for yy in y_peers:
+        gather_send(c, col_of(z, yy, k))
+    for zz in z_peers:
+        gather_send(c, col_of(zz, y, k))
+    gather_send(c, col_of(z, y, 1 - k))
+
     for copy in to_smem:
         copy.wait()
     for load in loads:
@@ -124,25 +124,17 @@
         sums[j + 1] = acc.astype(BF16)
         return acc
 
-    parts = 4
+    parts = 8
     acc = jnp.zeros((side, side), F32)
     for part in range(parts):
         acc = lax.fori_loop(part * slots // parts, (part + 1) * slots // parts, add_slot, acc,
-                            unroll=2)
-        if part == 1:
-            for zz in z_peers:
-                block = col_of(zz, y, k)
-                gather_wait(block)
-                for yy in y_peers:
-                    gather_send(block, col_of(z, yy, k))
-                gather_send(block, col_of(z, y, 1 - k))
-        if part == parts - 1:
-            for d in range(O):
-                zz = lax.rem(z + d, O)
-                for yy in y_peers:
-                    block = col_of(zz, yy, k)
-                    gather_wait(block)
-                    gather_send(block, col_of(z, y, 1 - k))
+                            unroll=4)
+        for zz in z_peers[part - 2:part - 1] if part > 1 else []:
+            block = col_of(zz, y, k)
+            gather_wait(block)
+            for yy in y_peers:
+                gather_send(block, col_of(z, yy, k))
+            gather_send(block, col_of(z, y, 1 - k))
 
     for d in range(1, R):
         peer = lax.rem(r + d, R)
@@ -194,6 +186,13 @@
         return carry
 
     lax.fori_loop(0, O * (I - 1), send_y, 0)
+
+    for d in range(O):
+        zz = lax.rem(z + d, O)
+        for yy in y_peers:
+            block = col_of(zz, yy, k)
+            gather_wait(block)
+            gather_send(block, col_of(z, y, 1 - k))
 
     for d in range(O):
         for e in range(I):
@@ -255,18 +254,29 @@
     term_out[...] = term.reshape(term_out.shape)
 
     def term_copy(t):
-        return remote(term_out.at[t], term_in.at[me], term_send.at[t], term_recv.at[me],
+        return remote(term_out.at[t], term_in.at[me], term_send.at[0], term_recv.at[0],
                       (t // C, lax.rem(t, C)))
 
-    def term_arrival(t):
-        return remote(term_out.at[0], term_in.at[t], term_send.at[0], term_recv.at[t], (r, c))
+    def bulk(count, send, recv):
+        part = term_in.at[pl.ds(0, count)]
+        return remote(part, part, send.at[0], recv.at[0], (r, c))
+
+    def arrived(count, send, recv):
+        bulk(count, send, recv).wait_recv()
+
+    def sent(count, send, recv):
+        bulk(count, send, recv).wait_send()
+
+    def by_role(act, send, recv):
+        if owners == n:
+            act(n - 1, send, recv)
+        else:
+            pl.when(me < owners)(lambda: act(owners - 1, send, recv))
+            pl.when(me >= owners)(lambda: act(owners, send, recv))
 
     def tot_copy(t):
-        return remote(total.at[me], total.at[me], tot_send.at[t], tot_recv.at[me],
+        return remote(total.at[me], total.at[me], tot_send.at[0], tot_recv.at[0],
                       (t // C, lax.rem(t, C)))
-
-    def tot_arrival(t):
-        return remote(total.at[t], total.at[t], tot_send.at[0], tot_recv.at[t], (r, c))
 
     def others(count, act):
         def body(d, carry):
@@ -278,11 +288,11 @@
                 def _():
                     act(t)
             return carry
-        lax.fori_loop(1, n, body, 0)
+        lax.fori_loop(1, n, body, 0, unroll=n - 1 if n <= 32 else 1)
 
     def own_part():
         term_in[me] = term_out[me]
-        others(n, lambda t: term_arrival(t).wait_recv())
+        arrived(n - 1, term_send, term_recv)
         total[me] = jnp.sum(term_in[...], axis=0) * (1.0 / math.sqrt(n * stretch))
         others(n, lambda t: tot_copy(t).start())
 
@@ -308,15 +318,21 @@
         return carry
 
     lax.fori_loop(0, O * (I - 1), drain_y, 0)
-    others(owners, lambda t: term_copy(t).wait_send())
-    others(owners, lambda t: tot_arrival(t).wait_recv())
+    by_role(sent, term_send, term_recv)
+    by_role(arrived, tot_send, tot_recv)
     grad_weight[...] = total[...].reshape(grad_weight.shape)
     if owners == n:
-        others(n, lambda t: tot_copy(t).wait_send())
+        sent(n - 1, tot_send, tot_recv)
     else:
         @pl.when(me < owners)
         def _():
-            others(n, lambda t: tot_copy(t).wait_send())
+            sent(n - 1, tot_send, tot_recv)
+
+
+def hand_over(a, b, c, x, y, z):
+    x[...] = a[...]
+    y[...] = b[...]
+    z[...] = c[...]
 
 
 def per_device(R, C, features, weight, tiles, slot_tile_row, tile_cols, live_tiles, cotangent):
@@ -362,16 +378,17 @@
         dma((gathers,)), dma((C,)),
         dma((half,)), dma((half,)), dma((half,)), dma((half,)),
         dma((O,)), dma((O,)), dma((R,)), dma((R,)),
-        dma((n,)), dma((n,)), dma((n,)), dma((n,)),
+        dma((1,)), dma((1,)), dma((1,)), dma((1,)),
     ]
     v = pl.BlockSpec(memory_space=pltpu.VMEM)
-    return pl.pallas_call(
-        functools.partial(kernel, (R, C, O, I)),
-        out_shape=(
+    shapes = (
             jax.ShapeDtypeStruct((stretch, out_width), BF16),
             jax.ShapeDtypeStruct((stretch, width), BF16),
             jax.ShapeDtypeStruct((width, out_width), F32),
-        ),
+        )
+    results = pl.pallas_call(
+        functools.partial(kernel, (R, C, O, I)),
+        out_shape=shapes,
         in_specs=[v, v, pl.BlockSpec(memory_space=pl.ANY), v, v,
                   pl.BlockSpec(memory_space=pltpu.SMEM), v],
         out_specs=(v, v, v),
@@ -380,6 +397,8 @@
             collective_id=0, has_side_effects=True, vmem_limit_bytes=60 * 1024 * 1024),
     )(features, weight, tiles.reshape(slots, side, side), slot_tile_row.reshape(1, slots),
       tile_cols.reshape(1, slots), live_tiles, cotangent)
+    return pl.pallas_call(hand_over, out_shape=shapes, in_specs=[v, v, v],
+                          out_specs=(v, v, v))(*results)
 
 
 def solution(mesh):

time: 53.3 us -> 46 us (0.86)
  local copies, waits for them, and re-layouts: 4.61 us -> 0 us
  Pallas kernels: 47.1 us -> 44.5 us
    unnamed x3 -> x0, local copies, waits for them, and re-layouts: 4.61 us -> none
    pallas_call x1 -> x2, Pallas kernels: 47.1 us -> 44.5 us  [the longest x1 42.8 us: per_device(): pl.pallas_call(functools.partial(kernel, (R, C, O, I)), out_shape=shapes,...]
where the time goes in v2:
time: 46 us; the launch traced here: 45.8 us
  Pallas kernels  44.5 us (97%)
  between operations  1.29 us (3%)
    pallas_call x1, Pallas kernels, per_device(): pl.pallas_call(functools.partial(kernel, (R, C, O, I)), out_shape=shapes,...  42.8 us
    pallas_call x1, Pallas kernels, per_device(): pl.pallas_call(hand_over, out_shape=shapes, in_specs=[v, v, v], out_specs...  1.73 us

profile of v2, /device:TPU:0, one launch (start us, length us, event | category | flops | bytes accessed | tf_op | source)
XLA Modules:
  0.0 45.8 jit_solution(12372457962171765858)
XLA Ops:
  1.3 42.8 %shard_map.94 = (bf16[256,128]{1,0:T(8,128)(2,1)}, bf16[256,256]{1,0:T(8,128)(2,1)}, f32[256,128]{1,0:T(8,128)}) custom-call(bf16[256,256]{1,0:T(8,128)(2,1)} %features.1, bf16[256,128]{1,0:T(8,128)(2,1)} %weight.1, bf16[320,128,128]{2,1,0:T(8,128)(2,1)} %bitcast.3, s32[1,320]{1,0:T(1,128)} %bitcast.4, s32[1,320]{1,0:T(1,128)} %bitcast.5, ...), custom_call_target="tpu_custom_call" | custom-call | tf_op jit(solution)/shard_map/pallas_call | solution.py:389
  44.1 1.7 %shard_map.95 = (bf16[256,128]{1,0:T(8,128)(2,1)}, bf16[256,256]{1,0:T(8,128)(2,1)}, f32[256,128]{1,0:T(8,128)}) custom-call(bf16[256,128]{1,0:T(8,128)(2,1)} %get-tuple-element.6.a, bf16[256,256]{1,0:T(8,128)(2,1)} %get-tuple-element.7.b, f32[256,128]{1,0:T(8,128)} %get-tuple-element.8.c), custom_call_target="tpu_custom_call" | custom-call | tf_op jit(solution)/shard_map/pallas_call | solution.py:400

commit v3 on v2

--- a/solution.py
+++ b/solution.py
@@ -194,28 +194,6 @@
             gather_wait(block)
             gather_send(block, col_of(z, y, 1 - k))
 
-    for d in range(O):
-        for e in range(I):
-            gather_wait(col_of(lax.rem(z + d, O), lax.rem(y + e, I), 1 - k))
-    group = 4 if C % 4 == 0 else 1
-
-    def forward(s):
-        def step(g, out):
-            for b in range(group):
-                out = out + jnp.dot(stretch_block(s, g * group + b), proj[g * group + b],
-                                    preferred_element_type=F32)
-            return out
-        return lax.fori_loop(0, C // group, step, jnp.zeros((stretch, proj.shape[2]), F32))
-
-    log_copies = []
-    for d in range(1, R):
-        peer = lax.rem(r + d, R)
-        log_out[d - 1] = forward(peer)
-        copy = remote(log_out.at[d - 1], log_in.at[r], log_send.at[d], log_recv.at[r], (peer, c))
-        copy.start()
-        log_copies.append(copy)
-    mine_log = forward(r)
-
     def summed(zz):
         m = zz * I + y
         value = back_block(2 * m + k)
@@ -236,13 +214,29 @@
                       (r, col_of(zz, y, k)))
         copy.start()
         z_copies.append(copy)
-    back_t = summed(z)
+    for d in range(O):
+        for e in range(I):
+            gather_wait(col_of(lax.rem(z + d, O), lax.rem(y + e, I), 1 - k))
+    group = 4 if C % 4 == 0 else 1
+
+    def forward(s):
+        def step(g, out):
+            for b in range(group):
+                out = out + jnp.dot(stretch_block(s, g * group + b), proj[g * group + b],
+                                    preferred_element_type=F32)
+            return out
+        return lax.fori_loop(0, C // group, step, jnp.zeros((stretch, proj.shape[2]), F32))
+
+    log_copies = []
     for d in range(1, R):
         peer = lax.rem(r + d, R)
-        remote(log_out.at[0], log_in.at[peer], log_send.at[0], log_recv.at[peer],
-               (peer, c)).wait_recv()
-        mine_log = mine_log + log_in[peer]
-    logits[...] = mine_log.astype(BF16)
+        log_out[d - 1] = forward(peer)
+        copy = remote(log_out.at[d - 1], log_in.at[r], log_send.at[d], log_recv.at[r], (peer, c))
+        copy.start()
+        log_copies.append(copy)
+    mine_log = forward(r)
+
+    back_t = summed(z)
     for zz in z_peers:
         remote(z_out.at[0], z_in.at[zz], z_send.at[0], z_recv.at[zz], (r, c)).wait_recv()
         back_t = back_t + z_in[zz].astype(F32)
@@ -299,6 +293,12 @@
     others(owners, lambda t: term_copy(t).start())
     grad_features[...] = lax.dot_general(
         back, weight[...], (((1,), (1,)), ((), ())), preferred_element_type=F32).astype(BF16)
+    for d in range(1, R):
+        peer = lax.rem(r + d, R)
+        remote(log_out.at[0], log_in.at[peer], log_send.at[0], log_recv.at[peer],
+               (peer, c)).wait_recv()
+        mine_log = mine_log + log_in[peer]
+    logits[...] = mine_log.astype(BF16)
     if owners == n:
         own_part()
     else:

time: 46 us -> 43.9 us (0.954)
  Pallas kernels: 44.5 us -> 42.4 us
    pallas_call x1, Pallas kernels: 42.8 us -> 40.7 us  [per_device(): pl.pallas_call(functools.partial(kernel, (R, C, O, I)), out_shape=shapes,...]
where the time goes in v3:
time: 43.9 us; the launch traced here: 43.7 us
  Pallas kernels  42.4 us (97%)
  between operations  1.29 us (3%)
    pallas_call x1, Pallas kernels, per_device(): pl.pallas_call(functools.partial(kernel, (R, C, O, I)), out_shape=shapes,...  40.7 us
    pallas_call x1, Pallas kernels, per_device(): pl.pallas_call(hand_over, out_shape=shapes, in_specs=[v, v, v], out_specs...  1.73 us

profile of v3, /device:TPU:0, one launch (start us, length us, event | category | flops | bytes accessed | tf_op | source)
XLA Modules:
  0.0 43.7 jit_solution(9093968641947120265)
XLA Ops:
  1.3 40.7 %shard_map.94 = (bf16[256,128]{1,0:T(8,128)(2,1)}, bf16[256,256]{1,0:T(8,128)(2,1)}, f32[256,128]{1,0:T(8,128)}) custom-call(bf16[256,256]{1,0:T(8,128)(2,1)} %features.1, bf16[256,128]{1,0:T(8,128)(2,1)} %weight.1, bf16[320,128,128]{2,1,0:T(8,128)(2,1)} %bitcast.3, s32[1,320]{1,0:T(1,128)} %bitcast.4, s32[1,320]{1,0:T(1,128)} %bitcast.5, ...), custom_call_target="tpu_custom_call" | custom-call | tf_op jit(solution)/shard_map/pallas_call | solution.py:389
  42.0 1.7 %shard_map.95 = (bf16[256,128]{1,0:T(8,128)(2,1)}, bf16[256,256]{1,0:T(8,128)(2,1)}, f32[256,128]{1,0:T(8,128)}) custom-call(bf16[256,128]{1,0:T(8,128)(2,1)} %get-tuple-element.6.a, bf16[256,256]{1,0:T(8,128)(2,1)} %get-tuple-element.7.b, f32[256,128]{1,0:T(8,128)} %get-tuple-element.8.c), custom_call_target="tpu_custom_call" | custom-call | tf_op jit(solution)/shard_map/pallas_call | solution.py:400

commit v4 on v3

--- a/solution.py
+++ b/solution.py
@@ -245,14 +245,14 @@
 
     owners = term_out.shape[0]
     rows = term_out.shape[1]
-    term_out[...] = term.reshape(term_out.shape)
+    term_out[...] = term.reshape(term_out.shape).astype(BF16)
 
     def term_copy(t):
         return remote(term_out.at[t], term_in.at[me], term_send.at[0], term_recv.at[0],
                       (t // C, lax.rem(t, C)))
 
     def bulk(count, send, recv):
-        part = term_in.at[pl.ds(0, count)]
+        part = (term_in if send is term_send else total).at[pl.ds(0, count)]
         return remote(part, part, send.at[0], recv.at[0], (r, c))
 
     def arrived(count, send, recv):
@@ -287,7 +287,7 @@
     def own_part():
         term_in[me] = term_out[me]
         arrived(n - 1, term_send, term_recv)
-        total[me] = jnp.sum(term_in[...], axis=0) * (1.0 / math.sqrt(n * stretch))
+        total[me] = jnp.sum(term_in[...].astype(F32), axis=0) * (1.0 / math.sqrt(n * stretch))
         others(n, lambda t: tot_copy(t).start())
 
     others(owners, lambda t: term_copy(t).start())
@@ -320,7 +320,7 @@
     lax.fori_loop(0, O * (I - 1), drain_y, 0)
     by_role(sent, term_send, term_recv)
     by_role(arrived, tot_send, tot_recv)
-    grad_weight[...] = total[...].reshape(grad_weight.shape)
+    grad_weight[...] = total[pl.ds(0, owners)].reshape(grad_weight.shape)
     if owners == n:
         sent(n - 1, tot_send, tot_recv)
     else:
@@ -371,9 +371,9 @@
         vmem((O,) + blk, BF16),
         vmem((max(R - 1, 1), stretch, out_width), F32),
         vmem((R, stretch, out_width), F32),
-        vmem((owners, rows, out_width), F32),
+        vmem((owners, rows, out_width), BF16),
+        vmem((n, rows, out_width), BF16),
         vmem((n, rows, out_width), F32),
-        vmem((owners, rows, out_width), F32),
         dma((chunks,)), dma((2,)), dma((R,)), dma((R,)),
         dma((gathers,)), dma((C,)),
         dma((half,)), dma((half,)), dma((half,)), dma((half,)),

time: 43.9 us -> 43.2 us (0.984)
  Pallas kernels: 42.4 us -> 41.8 us
    pallas_call x1, Pallas kernels: 40.7 us -> 40 us  [per_device(): pl.pallas_call(functools.partial(kernel, (R, C, O, I)), out_shape=shapes,...]
where the time goes in v4:
time: 43.2 us; the launch traced here: 43.1 us
  Pallas kernels  41.8 us (97%)
  between operations  1.29 us (3%)
    pallas_call x1, Pallas kernels, per_device(): pl.pallas_call(functools.partial(kernel, (R, C, O, I)), out_shape=shapes,...  40 us
    pallas_call x1, Pallas kernels, per_device(): pl.pallas_call(hand_over, out_shape=shapes, in_specs=[v, v, v], out_specs...  1.73 us

profile of v4, /device:TPU:0, one launch (start us, length us, event | category | flops | bytes accessed | tf_op | source)
XLA Modules:
  0.0 43.1 jit_solution(12762327344969330123)
XLA Ops:
  1.3 40.0 %shard_map.94 = (bf16[256,128]{1,0:T(8,128)(2,1)}, bf16[256,256]{1,0:T(8,128)(2,1)}, f32[256,128]{1,0:T(8,128)}) custom-call(bf16[256,256]{1,0:T(8,128)(2,1)} %features.1, bf16[256,128]{1,0:T(8,128)(2,1)} %weight.1, bf16[320,128,128]{2,1,0:T(8,128)(2,1)} %bitcast.3, s32[1,320]{1,0:T(1,128)} %bitcast.4, s32[1,320]{1,0:T(1,128)} %bitcast.5, ...), custom_call_target="tpu_custom_call" | custom-call | tf_op jit(solution)/shard_map/pallas_call | solution.py:389
  41.3 1.7 %shard_map.95 = (bf16[256,128]{1,0:T(8,128)(2,1)}, bf16[256,256]{1,0:T(8,128)(2,1)}, f32[256,128]{1,0:T(8,128)}) custom-call(bf16[256,128]{1,0:T(8,128)(2,1)} %get-tuple-element.6.a, bf16[256,256]{1,0:T(8,128)(2,1)} %get-tuple-element.7.b, f32[256,128]{1,0:T(8,128)} %get-tuple-element.8.c), custom_call_target="tpu_custom_call" | custom-call | tf_op jit(solution)/shard_map/pallas_call | solution.py:400
